TPU v7x, 128 devices: a whole 4x4x4 slice. The times are simulated.
128 devices in a mesh: dp: 16 (over x_lo, z, core), mp: 8 (over x_hi, y).
Axes of the slice: x: 4 (x_hi: 2, x_lo: 2; x = x_hi * 2 + x_lo), y: 4, z: 4, core: 2. Of those that a mesh axis runs over, the one named last changes fastest.
Arguments:
- tokens: bfloat16 [8192, 1280], P('dp'), may hold values from -6 to 6
- norm_gain: float32 [1280], replicated, may hold values from 0.25 to 1.75
- widen_weight: bfloat16 [1280, 5120], P(None, 'mp'), may hold values from -0.15625 to 0.15625
- narrow_weight: bfloat16 [5120, 1280], P('mp'), may hold values from -0.078125 to 0.078125
- final_gain: float32 [1280], replicated, may hold values from 0.25 to 1.75
- adaptor_in: bfloat16 [3, 1280, 1280], P(None, None, 'mp'), may hold values from -0.15625 to 0.15625
- head_dino: bfloat16 [1280, 1536], P('mp'), may hold values from -0.15625 to 0.15625
- head_siglip: bfloat16 [1280, 1152], P('mp'), may hold values from -0.15625 to 0.15625
- head_sam: bfloat16 [1280, 1280], P('mp'), may hold values from -0.15625 to 0.15625
- teacher_dino: bfloat16 [2, 8192, 1536], P(None, 'dp', 'mp'), may hold values from -6 to 6
- teacher_siglip: bfloat16 [2, 8192, 1152], P(None, 'dp', 'mp'), may hold values from -6 to 6
- teacher_sam: bfloat16 [2, 8192, 1280], P(None, 'dp', 'mp'), may hold values from -6 to 6
- step_lags: int32 [3], replicated, may hold values from 1 to 2, as said below
- owner_slot: int32 [256], replicated, may hold values from 0 to 255, as said below
Outputs:
- grad_widen: float32 [5120, 1280], P('mp', 'dp')
- grad_narrow: float32 [5120, 1280], P('mp', 'dp')
- grad_adaptor: float32 [3, 1280, 1280], P(None, 'dp', 'mp')
- grad_dino: float32 [1280, 1536], P('mp', 'dp')
- grad_siglip: float32 [1280, 1152], P('mp', 'dp')
- grad_sam: float32 [1280, 1280], P('mp', 'dp')
Inputs may be any that keep to these rules, and one draw needn't show every extreme that they name: owner_slot is a permutation; of the 16 images in each aligned block of 16 images, exactly 1 have slots in each aligned block of 16 slots. `step_lags`: the three lags are not all equal.
All inputs are finite; a program needn't handle non-finite values.
Results may differ from a plain program's by a relative error of at most 0.02.
Values may be sent and summed in bfloat16 or wider, within the bound.
A program may use at most 128 MiB of HBM per device.

v0:
```python
import jax
import jax.numpy as jnp
from jax import lax
from jax.sharding import PartitionSpec as P

PATCH = 32
slope_coef = 0.7978845608028654
cubic_coef = 0.044715


def in_one_piece(arrays, axis, split_dim, concat_dim, along):
    widths = [a.shape[along] for a in arrays]
    both = jnp.concatenate(arrays, axis=along)
    filled = lax.all_to_all(both, axis, split_axis=split_dim, concat_axis=concat_dim, tiled=True)
    return tuple(jnp.split(filled, [sum(widths[:k]) for k in range(1, len(widths))], axis=along))


def from_everyone(shard, axis):
    size = lax.axis_size(axis)
    return lax.all_to_all(
        jnp.broadcast_to(shard[None], (size, *shard.shape)), axis, 0, 0, tiled=True
    )


def taken_together(shard, axis):
    everything = from_everyone(shard, axis)
    return jnp.sum(everything, axis=0)


def joined_along(pieces, dim):
    shape = list(pieces.shape[1:])
    shape[dim] *= pieces.shape[0]
    return jnp.moveaxis(pieces, 0, dim).reshape(shape)


def gather_packed(arrays, axis, dims):
    vector = jnp.concatenate([a.reshape(-1) for a in arrays])
    lines, at, done = (lax.all_gather(vector, axis), 0, [])
    for a, dim in zip(arrays, dims):
        pieces = lines[:, at : at + a.size].reshape(-1, *a.shape)
        done.append(joined_along(pieces, dim))
        at += a.size
    return tuple(done)


def for_sending(shard):
    return jax.tree.map(lambda a: a.astype(jnp.bfloat16) if a.dtype == jnp.float32 else a, shard)


def in_blocks(shard, dim, size):
    shape = shard.shape
    pieces = shard.reshape(*shape[:dim], size, shape[dim] // size, *shape[dim + 1 :])
    return jnp.moveaxis(pieces, dim, 0)


def sent_and_summed(shard, axis, dim):
    pieces = in_blocks(shard, dim, lax.axis_size(axis))
    arrived = lax.all_to_all(pieces, axis, split_axis=0, concat_axis=0, tiled=True)
    return arrived.astype(jnp.float32).sum(axis=0)


def collect(shard, axis, dim):
    return joined_along(from_everyone(shard, axis), dim)


def side_by_side(arrays, axis, dim, along):
    widths = [a.shape[along] for a in arrays]
    both = jnp.concatenate(arrays, axis=along)
    filled = lax.psum_scatter(both, axis, scatter_dimension=dim, tiled=True)
    return tuple(jnp.split(filled, [sum(widths[:k]) for k in range(1, len(widths))], axis=along))


def smooth(value):
    return 0.5 * value * (1.0 + jnp.tanh(slope_coef * (value + cubic_coef * value * value * value)))


def smooth_slope(value):
    tangent = jnp.tanh(slope_coef * (value + cubic_coef * value * value * value))
    return 0.5 * (1.0 + tangent) + 0.5 * value * (1.0 - tangent * tangent) * slope_coef * (
        1.0 + 3.0 * cubic_coef * value * value
    )


def normalize(value, gain):
    centre = value - jnp.mean(value, axis=-1, keepdims=True)
    inverse = lax.rsqrt(jnp.mean(centre * centre, axis=-1, keepdims=True) + 1e-06)
    normal = centre * inverse
    return (normal * gain, normal, inverse)


def normalize_back(upstream, gain, normal, inverse):
    scaled = upstream * gain
    return inverse * (
        scaled
        - jnp.mean(scaled, axis=-1, keepdims=True)
        - normal * jnp.mean(scaled * normal, axis=-1, keepdims=True)
    )


def finish(product, square_student, square_target, student, target):
    joint = lax.rsqrt(square_student * square_target)
    cosine = product * joint
    slope = cosine[:, None] * student / square_student[:, None] - target * joint[:, None]
    return (cosine, slope)


def column_terms(students, targets):
    return jnp.stack(
        [
            jnp.stack(
                [
                    jnp.sum(students[index] * targets[index], axis=-1),
                    jnp.sum(students[index] * students[index], axis=-1),
                    jnp.sum(targets[index] * targets[index], axis=-1),
                ]
            )
            for index in range(3)
        ]
    )


def column_finish(summed_terms, students, targets):
    local_slopes = []
    for index in range(3):
        cosine, slope = finish(
            summed_terms[index, 0],
            summed_terms[index, 1] + 1e-06,
            summed_terms[index, 2] + 1e-06,
            students[index],
            targets[index],
        )
        local_slopes.append(slope.astype(jnp.bfloat16))
    return local_slopes


def local(
    tokens,
    norm_gain,
    widen_weight,
    narrow_weight,
    final_gain,
    adaptor_in,
    head_dino,
    head_siglip,
    head_sam,
    teacher_dino,
    teacher_siglip,
    teacher_sam,
    step_lags,
    owner_slot,
):
    groups = lax.axis_size("dp")
    members = lax.axis_size("mp")
    group = lax.axis_index("dp")
    member = lax.axis_index("mp")
    rows = tokens.shape[0]
    images = rows // PATCH
    share = images // groups
    block = rows // members
    heads = (head_dino, head_siglip, head_sam)
    mine = lax.dynamic_slice_in_dim(owner_slot, group * images, images)
    sending = jnp.argsort(mine)
    outgoing = []
    for index, teacher in enumerate((teacher_dino, teacher_siglip, teacher_sam)):
        stale = lax.dynamic_index_in_dim(teacher, step_lags[index] - 1, 0, keepdims=False)
        width = stale.shape[-1]
        ordered = jnp.take(stale.reshape(images, PATCH, width), sending, axis=0)
        outgoing.append(ordered)
    arrived = in_one_piece((outgoing[0], outgoing[1], outgoing[2]), "dp", 0, 0, 2)
    ranked = jnp.sort(owner_slot.reshape(groups, images), axis=1)
    landed = (
        lax.dynamic_slice_in_dim(ranked, group * share, share, 1).reshape(images) - group * images
    )
    placing = jnp.argsort(landed)
    owned = [jnp.take(piece, placing, axis=0) for piece in arrived]
    first, normal_one, inverse_one = normalize(tokens.astype(jnp.float32), norm_gain)
    first = first.astype(jnp.bfloat16)
    widened = jnp.dot(first, widen_weight, preferred_element_type=jnp.float32)
    active = smooth(widened).astype(jnp.bfloat16)
    mixed = jnp.dot(active, narrow_weight, preferred_element_type=jnp.float32)
    hidden = tokens.astype(jnp.float32) + lax.psum(mixed, "mp")
    final, normal_two, inverse_two = normalize(hidden, final_gain)
    final = final.astype(jnp.bfloat16)
    before = jnp.einsum("rd,tdh->trh", final, adaptor_in, preferred_element_type=jnp.float32)
    lifted = smooth(before).astype(jnp.bfloat16)
    targets = [piece.reshape(rows, piece.shape[-1]).astype(jnp.float32) for piece in owned]
    whole_lifted = lax.all_gather(lifted, "mp", axis=2, tiled=True)
    head_columns = (
        lax.all_to_all(head_dino, "mp", split_axis=1, concat_axis=0, tiled=True),
        lax.all_to_all(head_siglip, "mp", split_axis=1, concat_axis=0, tiled=True),
        lax.all_to_all(head_sam, "mp", split_axis=1, concat_axis=0, tiled=True),
    )
    students = [
        jnp.dot(whole_lifted[index], head_columns[index], preferred_element_type=jnp.float32)
        for index in range(3)
    ]
    summed_terms = taken_together(column_terms(students, targets), "mp")
    local_slopes = column_finish(summed_terms, students, targets)
    slopes = gather_packed((local_slopes[0], local_slopes[1], local_slopes[2]), "mp", (1, 1, 1))
    column_grads = tuple(
        (
            jnp.einsum(
                "rh,rc->hc",
                whole_lifted[index],
                local_slopes[index],
                preferred_element_type=jnp.float32,
            )
            for index in range(3)
        )
    )
    head_grads = list(
        jax.tree.map(
            lambda part, own: part.astype(own.dtype),
            lax.all_to_all(
                for_sending(column_grads), "mp", split_axis=0, concat_axis=1, tiled=True
            ),
            column_grads,
        )
    )
    back = jnp.stack(
        [
            jnp.einsum("rc,hc->rh", slopes[index], heads[index], preferred_element_type=jnp.float32)
            for index in range(3)
        ]
    )
    inner = (back * smooth_slope(before)).astype(jnp.bfloat16)
    grad_adaptor = jnp.einsum("rd,trh->tdh", final, inner, preferred_element_type=jnp.float32)
    upstream_part = jnp.einsum("trh,tdh->rd", inner, adaptor_in, preferred_element_type=jnp.float32)
    upstream = sent_and_summed(upstream_part.astype(jnp.bfloat16), "mp", 0)
    normal_rows = lax.dynamic_slice_in_dim(normal_two, member * block, block, 0)
    inverse_rows = lax.dynamic_slice_in_dim(inverse_two, member * block, block, 0)
    through_rows = normalize_back(upstream, final_gain, normal_rows, inverse_rows).astype(
        jnp.bfloat16
    )
    through = collect(through_rows, "mp", 0)
    grad_narrow = jnp.einsum("rf,rd->fd", active, through, preferred_element_type=jnp.float32)
    back_two = jnp.einsum("rd,fd->rf", through, narrow_weight, preferred_element_type=jnp.float32)
    inner_two = (back_two * smooth_slope(widened)).astype(jnp.bfloat16)
    grad_widen = jnp.einsum("rf,rd->fd", inner_two, first, preferred_element_type=jnp.float32)
    reduced = (
        *tuple(
            (
                part.astype(jnp.float32)
                for part in side_by_side(
                    (grad_widen.astype(jnp.bfloat16), grad_narrow.astype(jnp.bfloat16)), "dp", 1, 0
                )
            )
        ),
        lax.psum_scatter(
            grad_adaptor.astype(jnp.bfloat16), "dp", scatter_dimension=1, tiled=True
        ).astype(jnp.float32),
        lax.psum_scatter(
            head_grads[0].astype(jnp.bfloat16), "dp", scatter_dimension=1, tiled=True
        ).astype(jnp.float32),
        lax.psum_scatter(
            head_grads[1].astype(jnp.bfloat16), "dp", scatter_dimension=1, tiled=True
        ).astype(jnp.float32),
        lax.psum_scatter(
            head_grads[2].astype(jnp.bfloat16), "dp", scatter_dimension=1, tiled=True
        ).astype(jnp.float32),
    )
    return (reduced[0], reduced[1], reduced[2], reduced[3], reduced[4], reduced[5])


def solution(mesh):
    placed = (
        P("dp", None),
        P(),
        P(None, "mp"),
        P("mp", None),
        P(),
        P(None, None, "mp"),
        P("mp", None),
        P("mp", None),
        P("mp", None),
        P(None, "dp", "mp"),
        P(None, "dp", "mp"),
        P(None, "dp", "mp"),
        P(),
        P(),
    )
    return jax.shard_map(
        local,
        mesh=mesh,
        in_specs=placed,
        out_specs=(
            P("mp", "dp"),
            P("mp", "dp"),
            P(None, "dp", "mp"),
            P("mp", "dp"),
            P("mp", "dp"),
            P("mp", "dp"),
        ),
        check_vma=False,
    )
```

profile of v0, /device:TPU:0, one launch (start us, length us, event | category | flops | bytes accessed | tf_op | source)
XLA Modules:
  0.0 680.4 jit_solution(16795986844906720179)
XLA Ops:
  9.5 2.7 fusion.40
  13.3 2.9 fusion.38
  16.3 98.4 %all-reduce.2.cloned.1.call-done = f32[512,1280]{1,0:T(8,128)} async-done(((f32[512,1280]{1,0:T(8,128)}), f32[512,1280]{1,0:T(8,128)}) %all-reduce.2.cloned.1.call-update) | async-done | bytes 2621456 | tf_op jit(solution)/shard_map/psum | solution.py:181
  123.1 3.7 all-to-all-start.2
  169.9 7.2 %all-to-all-start.3 = ((bf16[160,8,160]{0,2,1:T(8,128)(2,1)}), bf16[160,8,160]{0,2,1:T(8,128)(2,1)}, u32[]{:S(2)}, u32[]{:S(2)}) async-start(bf16[160,8,160]{0,2,1:T(8,128)(2,1)} %bitcast.150), calls=%async_computation.3 | async-start | bytes 1310720 | tf_op jit(solution)/shard_map/all_to_all | solution.py:191
  180.3 8.3 %all-to-all-done.3 = bf16[160,8,160]{0,2,1:T(8,128)(2,1)} async-done(((bf16[160,8,160]{0,2,1:T(8,128)(2,1)}), bf16[160,8,160]{0,2,1:T(8,128)(2,1)}, u32[]{:S(2)}, u32[]{:S(2)}) %all-to-all-start.3) | async-done | bytes 409632 | tf_op jit(solution)/shard_map/all_to_all | solution.py:191
  188.6 4.5 all-to-all-start.1
  204.0 5.2 all-to-all-start
  228.6 2.6 multiply_reduce_fusion.8
  231.3 2.7 multiply_reduce_fusion.5
  236.5 15.4 %all_to_all.134 = f32[8,3,3,512]{3,2,1,0:T(4,128)S(1)} all-to-all(f32[8,3,3,512]{3,2,1,0:T(4,128)S(1)} %broadcast_in_dim.31), channel_id=1, replica_groups=mesh['dp'=16,'mp'=8] {'mp'}, dimensions={0} | all-to-all | bytes 294912 | tf_op jit(solution)/shard_map/all_to_all | solution.py:20
  265.7 2.6 convolution_convert_fusion.5
  271.0 3.6 all-to-all-start.8
  274.5 2.7 convolution_convert_fusion.3
  279.3 2.6 convolution_convert_fusion.4
  282.0 2.7 all_to_all.120
  286.7 2.6 all-to-all-done.8
  289.2 4.6 all-to-all-start.9
  294.4 41.7 %all-gather.6.cloned.1.call-done = bf16[2031616]{0:T(1024)(128)(2,1)} async-done(((bf16[253952]{0:T(1024)(128)(2,1)}), bf16[2031616]{0:T(1024)(128)(2,1)}) %all-gather.6.cloned.1.call-update) | async-done | bytes 4063248 | tf_op jit(solution)/shard_map/all_gather | solution.py:38
  336.1 5.8 reshape.330
  344.2 2.5 slice.101
  346.8 2.7 slice.99
  349.4 2.8 reshape.363
  352.3 5.2 reshape.273
  357.5 3.7 copy.154
  361.2 3.3 reshape.365
  364.5 3.0 reshape.361
  367.5 4.1 reshape.271
  371.6 3.9 copy.153
  375.5 4.6 reshape.275
  380.0 3.8 copy.155
  383.9 2.6 convolution_bitcast_fusion.1
  389.1 4.2 all-to-all-start.7
  397.5 7.8 %all-to-all-done.7 = bf16[8,160,192]{2,1,0:T(8,128)(2,1)} async-done(((bf16[8,160,192]{2,1,0:T(8,128)(2,1)}), bf16[8,160,192]{2,1,0:T(8,128)(2,1)}, u32[]{:S(2)}, u32[]{:S(2)}) %all-to-all-start.7) | async-done | bytes 491552 | tf_op jit(solution)/shard_map/all_to_all | solution.py:214
  405.3 4.3 all-to-all-start.5
  413.3 13.9 %all-to-all-done.5 = bf16[8,64,1280]{2,1,0:T(8,128)(2,1)} async-done(((bf16[8,64,1280]{2,1,0:T(8,128)(2,1)}), bf16[8,64,1280]{2,1,0:T(8,128)(2,1)}, u32[]{:S(2)}, u32[]{:S(2)}) %all-to-all-start.5) | async-done | bytes 1310752 | tf_op jit(solution)/shard_map/all_to_all | solution.py:58
  432.1 4.4 all-to-all-start.6
  436.8 3.6 fusion.3
  440.4 4.9 copy.167
  445.3 6.0 reshape.355
  451.4 4.4 all-to-all-done.6
  455.8 4.0 convolution_convert_fusion
  459.9 5.8 convolution_convert_fusion.1
  465.7 3.9 pad_maximum_fusion
  469.6 5.7 copy.165
  478.5 61.3 %reduce-scatter.20.cloned.1.call-done = bf16[96,160]{1,0:T(8,128)(2,1)} async-done(((bf16[1536,160]{1,0:T(8,128)(2,1)}), bf16[96,160]{1,0:T(8,128)(2,1)}) %reduce-scatter.20.cloned.1.call-update) | async-done | bytes 30736
  541.3 62.2 %reduce-scatter.18.cloned.1.call-done = bf16[80,480]{1,0:T(8,128)(2,1)} async-done(((bf16[1280,480]{1,0:T(8,128)(2,1)}), bf16[80,480]{1,0:T(8,128)(2,1)}) %reduce-scatter.18.cloned.1.call-update) | async-done | bytes 76816
  605.6 64.9 %reduce-scatter.16.cloned.1.call-done = bf16[80,1280]{1,0:T(8,128)(2,1)} async-done(((bf16[1280,1280]{1,0:T(8,128)(2,1)}), bf16[80,1280]{1,0:T(8,128)(2,1)}) %reduce-scatter.16.cloned.1.call-update) | async-done | bytes 204816
  (210 shorter events, 135.7 us)
Async XLA Ops:
  7.2 6.1 copy-start
  7.2 1.8 copy-start.1
  7.2 2.3 copy-start.31
  7.2 107.5 %all-reduce.2.cloned.1.call-start = ((), (), s32[]{:S(2)}) async-start(), calls=%async_computation.15 | async-start | bytes 5242880 | tf_op jit(solution)/shard_map/psum | solution.py:181
  9.0 3.2 copy-start.24
  9.5 2.7 copy-start.28
  16.3 212.3 %all-gather.4.cloned.1.call-start = ((), (), s32[]{:S(2)}) async-start(), calls=%async_computation.16 | async-start | bytes 4423680 | tf_op jit(solution)/shard_map/all_gather | solution.py:187
  114.7 2.5 copy-start.3
  117.8 1.3 copy-start.16
  118.4 1.6 copy-start.2
  120.0 2.1 copy-start.14
  122.0 4.8 copy-start.27
  122.0 9.3 %copy-start.30 = (s32[256]{0:T(256)S(1)}, s32[256]{0:T(256)}, u32[]{:S(2)}) copy-start(s32[256]{0:T(256)} %param.33) | copy-start | bytes 3076
  123.1 46.8 %all-to-all-start.2 = ((bf16[160,8,144]{0,2,1:T(8,128)(2,1)}), bf16[160,8,144]{0,2,1:T(8,128)(2,1)S(1)}, u32[]{:S(2)}, u32[]{:S(2)}) async-start(bf16[160,8,144]{0,2,1:T(8,128)(2,1)} %bitcast.153), calls=%async_computation.2 | async-start | bytes 1179648 | tf_op jit(solution)/shard_map/all_to_all | solution.py:190
  169.9 10.4 %copy-start.8 = (bf16[160,8,144]{0,2,1:T(8,128)(2,1)}, bf16[160,8,144]{0,2,1:T(8,128)(2,1)S(1)}, u32[]{:S(2)}) copy-start(bf16[160,8,144]{0,2,1:T(8,128)(2,1)S(1)} %all-to-all-done.2) | copy-start | bytes 1105924
  169.9 18.7 %all-to-all-start.3 = ((bf16[160,8,160]{0,2,1:T(8,128)(2,1)}), bf16[160,8,160]{0,2,1:T(8,128)(2,1)}, u32[]{:S(2)}, u32[]{:S(2)}) async-start(bf16[160,8,160]{0,2,1:T(8,128)(2,1)} %bitcast.150), calls=%async_computation.3 | async-start | bytes 1310720 | tf_op jit(solution)/shard_map/all_to_all | solution.py:191
  178.2 15.0 %copy-start.33 = (s32[16]{0:T(128)S(1)}, s32[16]{0:T(128)}, u32[]{:S(2)}) copy-start(s32[16]{0:T(128)} %get-tuple-element.15) | copy-start | bytes 196
  188.6 15.4 %all-to-all-start.1 = ((bf16[16,32,496]{2,1,0:T(8,128)(2,1)}), bf16[16,32,496]{2,1,0:T(8,128)(2,1)S(1)}, u32[]{:S(2)}, u32[]{:S(2)}) async-start(bf16[16,32,496]{2,1,0:T(8,128)(2,1)} %pad_maximum_fusion.1), calls=%async_computation.1 | async-start | bytes 1048576 | tf_op jit(solution)/shard_map/all_to_all | solution.py:14
  204.0 27.3 %all-to-all-start = ((bf16[160,8,192]{2,0,1:T(8,128)(2,1)}), bf16[160,8,192]{2,0,1:T(8,128)(2,1)}, u32[]{:S(2)}, u32[]{:S(2)}) async-start(bf16[160,8,192]{2,0,1:T(8,128)(2,1)} %copy.134), calls=%async_computation | async-start | bytes 1310720 | tf_op jit(solution)/shard_map/all_to_all | solution.py:189
  209.2 127.0 %all-gather.6.cloned.1.call-start = ((), (), s32[]{:S(2)}) async-start(), calls=%async_computation.18 | async-start | bytes 4571136 | tf_op jit(solution)/shard_map/all_gather | solution.py:38
  216.6 5.7 copy-start.9
  223.5 4.2 copy-start.10
  228.6 2.7 copy-start.13
  231.3 2.8 copy-start.18
  231.3 2.8 copy-start.22
  254.6 2.8 copy-start.21
  258.6 2.9 copy-start.20
  262.6 3.1 copy-start.19
  271.0 18.3 %all-to-all-start.8 = ((bf16[8,160,144]{1,2,0:T(8,128)(2,1)}), bf16[8,160,144]{1,2,0:T(8,128)(2,1)S(1)}, u32[]{:S(2)}, u32[]{:S(2)}) async-start(bf16[8,160,144]{1,2,0:T(8,128)(2,1)} %copy.158), calls=%async_computation.8 | async-start | bytes 1179648 | tf_op jit(solution)/shard_map/all_to_all | solution.py:214
  289.2 4.8 copy-start.7
  289.2 99.9 %all-to-all-start.9 = ((bf16[8,160,160]{1,2,0:T(8,128)(2,1)}), bf16[8,160,160]{1,2,0:T(8,128)(2,1)}, u32[]{:S(2)}, u32[]{:S(2)}) async-start(bf16[8,160,160]{1,2,0:T(8,128)(2,1)} %copy.159), calls=%async_computation.10 | async-start | bytes 1310720 | tf_op jit(solution)/shard_map/all_to_all | solution.py:214
  293.8 181.4 %reduce-scatter.14.cloned.1.call-start = ((), (), s32[]{:S(2)}) async-start(), calls=%async_computation.17 | async-start | bytes 626688 | tf_op jit(solution)/shard_map/reduce_scatter | solution.py:255
  380.0 3.8 copy-start.12
  383.8 2.6 copy-start.6
  383.8 2.6 copy-start.15
  383.9 3.7 copy-start.11
  386.4 1.5 copy-start.5
  389.1 16.1 %all-to-all-start.7 = ((bf16[8,160,192]{2,1,0:T(8,128)(2,1)}), bf16[8,160,192]{2,1,0:T(8,128)(2,1)}, u32[]{:S(2)}, u32[]{:S(2)}) async-start(bf16[8,160,192]{2,1,0:T(8,128)(2,1)} %bitcast.149), calls=%async_computation.7 | async-start | bytes 1310720 | tf_op jit(solution)/shard_map/all_to_all | solution.py:214
  393.3 2.2 copy-start.17
  405.3 21.9 %all-to-all-start.5 = ((bf16[8,64,1280]{2,1,0:T(8,128)(2,1)}), bf16[8,64,1280]{2,1,0:T(8,128)(2,1)}, u32[]{:S(2)}, u32[]{:S(2)}) async-start(bf16[8,64,1280]{2,1,0:T(8,128)(2,1)} %bitcast.157), calls=%async_computation.5 | async-start | bytes 2621440 | tf_op jit(solution)/shard_map/all_to_all | solution.py:58
  409.5 67.4 %reduce-scatter.22.cloned.1.call-start = ((), (), s32[]{:S(2)}) async-start(), calls=%async_computation.22 | async-start | bytes 696320
  410.1 129.6 %reduce-scatter.20.cloned.1.call-start = ((), (), s32[]{:S(2)}) async-start(), calls=%async_computation.21 | async-start | bytes 835584
  432.1 23.7 %all-to-all-start.6 = ((bf16[8,64,1280]{2,1,0:T(8,128)(2,1)}), bf16[8,64,1280]{2,1,0:T(8,128)(2,1)}, u32[]{:S(2)}, u32[]{:S(2)}) async-start(bf16[8,64,1280]{2,1,0:T(8,128)(2,1)} %broadcast_in_dim.32), calls=%async_computation.6 | async-start | bytes 2621440 | tf_op jit(solution)/shard_map/all_to_all | solution.py:20
  436.6 166.9 %reduce-scatter.18.cloned.1.call-start = ((), (), s32[]{:S(2)}) async-start(), calls=%async_computation.20 | async-start | bytes 1392640
  451.4 219.1 %reduce-scatter.16.cloned.1.call-start = ((), (), s32[]{:S(2)}) async-start(), calls=%async_computation.19 | async-start | bytes 3481600
  455.8 4.1 copy-start.25
  455.8 4.1 copy-start.29
  455.8 4.1 copy-start.32
  (4 other events, 3.9 us)
Sparse Core Ops, SparseCore 0:
  16.4 98.3 all-reduce.1
  122.2 70.8 all-gather.3
  265.8 70.2 all-gather.5
  338.3 59.7 reduce-scatter.13
  412.4 64.5 reduce-scatter.21
  479.2 60.5 reduce-scatter.19
  542.1 61.3 reduce-scatter.17
  605.9 64.4 reduce-scatter.15
where the time goes:
time: 692 us; the launch traced here: 680 us
  waiting for transfers between devices  368 us (53%)
  local copies, waits for them, and re-layouts  147 us (21%)
  other arithmetic  45.7 us (7%)
  starting transfers between devices  42.8 us (6%)
  matrix products  42.4 us (6%)
  between operations  18.8 us (3%)
  blocking collectives  15.4 us (2%)
    unnamed x12, waiting for transfers between devices  190 us
    psum x1, waiting for transfers between devices, local(): hidden = tokens.astype(jnp.float32) + lax.psum(mixed, 'mp')  98.4 us
    unnamed x90, local copies, waits for them, and re-layouts  44.9 us
    all_gather x1, waiting for transfers between devices, gather_packed(): lines, at, done = (lax.all_gather(vector, axis), 0, [])  41.7 us
    all_to_all x1, blocking collectives, from_everyone(): lax.all_to_all(jnp.broadcast_to(shard[None], (size, *shard.shape)), axis,...  15.4 us
    reshape x3, local copies, waits for them, and re-layouts, gather_packed(): pieces = lines[:, at:at + a.size].reshape(-1, *a.shape)  13.9 us
    all_to_all x1, waiting for transfers between devices, sent_and_summed(): lax.all_to_all(pieces, axis, split_axis=0, concat_axis=0, tiled=True)  13.9 us
  transfers between devices with their start and end apart: 17, of which 12 were waited for; matrix products, arithmetic and copies ran while one was open for 27% of the time, Pallas kernels for 0%

commit v1 on v0

--- a/solution.py
+++ b/solution.py
@@ -178,7 +178,7 @@
     widened = jnp.dot(first, widen_weight, preferred_element_type=jnp.float32)
     active = smooth(widened).astype(jnp.bfloat16)
     mixed = jnp.dot(active, narrow_weight, preferred_element_type=jnp.float32)
-    hidden = tokens.astype(jnp.float32) + lax.psum(mixed, "mp")
+    hidden = tokens.astype(jnp.float32) + jnp.sum(lax.all_gather(mixed, "mp"), axis=0)
     final, normal_two, inverse_two = normalize(hidden, final_gain)
     final = final.astype(jnp.bfloat16)
     before = jnp.einsum("rd,tdh->trh", final, adaptor_in, preferred_element_type=jnp.float32)

time: 692 us -> 833 us (1.20)
  waiting for transfers between devices: 368 us -> 493 us
  other arithmetic: 45.7 us -> 57 us
    all_gather x0 -> x1, waiting for transfers between devices: none -> 223 us  [local(): lax.all_gather(mixed, 'mp')]
    psum x1 -> x0, waiting for transfers between devices: 98.4 us -> none  [local(): hidden = tokens.astype(jnp.float32) + lax.psum(mixed, 'mp')]
    reduce_sum x0 -> x1, other arithmetic: none -> 9.67 us  [local(): jnp.sum(lax.all_gather(mixed, 'mp'), axis=0)]
    unnamed x90 -> x84, local copies, waits for them, and re-layouts: 44.9 us -> 44.5 us
  transfers between devices with their start and end apart: 17 -> 17, of which waited for: 12 -> 12; matrix products, arithmetic and copies ran while one was open for 27% -> 23% of each run, Pallas kernels for 0% -> 0%
where the time goes in v1:
time: 833 us; the launch traced here: 820 us
  waiting for transfers between devices  493 us (59%)
  local copies, waits for them, and re-layouts  148 us (18%)
  other arithmetic  57 us (7%)
  starting transfers between devices  44.4 us (5%)
  matrix products  44 us (5%)
  between operations  18.8 us (2%)
  blocking collectives  15.4 us (2%)
    all_gather x1, waiting for transfers between devices, local(): lax.all_gather(mixed, 'mp')  223 us
    unnamed x12, waiting for transfers between devices  190 us
    unnamed x84, local copies, waits for them, and re-layouts  44.5 us
    all_gather x1, waiting for transfers between devices, gather_packed(): lines, at, done = (lax.all_gather(vector, axis), 0, [])  41.6 us
  transfers between devices with their start and end apart: 17, of which 12 were waited for; matrix products, arithmetic and copies ran while one was open for 23% of the time, Pallas kernels for 0%

profile of v1, /device:TPU:0, one launch (start us, length us, event | category | flops | bytes accessed | tf_op | source)
XLA Modules:
  0.0 820.4 jit_solution(11540051557518972166)
XLA Ops:
  9.5 2.7 fusion.40
  13.3 2.9 fusion.38
  16.3 222.6 %all-gather.8.cloned.1.call-done = f32[4096,1280]{1,0:T(8,128)} async-done(((f32[512,1280]{1,0:T(8,128)}), f32[4096,1280]{1,0:T(8,128)}) %all-gather.8.cloned.1.call-update) | async-done | bytes 20971536 | tf_op jit(solution)/shard_map/all_gather | solution.py:181
  238.9 9.7 %reduce_sum.164 = f32[512,1280]{1,0:T(8,128)} reduce(f32[8,512,1280]{2,1,0:T(8,128)} %bitcast.139, f32[]{:T(128)} %constant.49.clone.1), dimensions={0}, to_apply=%region_2.3 | reduce | flops 4587520 | bytes 23592964 | tf_op jit(solution)/shard_map/reduce_sum | solution.py:181
  257.0 3.5 all-to-all-start.2
  304.4 7.1 all-to-all-start.3
  314.7 8.7 %all-to-all-done.3 = bf16[160,8,160]{0,2,1:T(8,128)(2,1)} async-done(((bf16[160,8,160]{0,2,1:T(8,128)(2,1)}), bf16[160,8,160]{0,2,1:T(8,128)(2,1)}, u32[]{:S(2)}, u32[]{:S(2)}) %all-to-all-start.3) | async-done | bytes 409632 | tf_op jit(solution)/shard_map/all_to_all | solution.py:191
  323.5 4.7 all-to-all-start.1
  335.0 2.5 all_to_all.108
  339.0 6.8 all-to-all-start
  366.0 2.6 multiply_reduce_fusion.8
  368.7 2.8 multiply_reduce_fusion.5
  374.0 15.4 %all_to_all.134 = f32[8,3,3,512]{3,2,1,0:T(4,128)S(1)} all-to-all(f32[8,3,3,512]{3,2,1,0:T(4,128)S(1)} %broadcast_in_dim.31), channel_id=1, replica_groups=mesh['dp'=16,'mp'=8] {'mp'}, dimensions={0} | all-to-all | bytes 294912 | tf_op jit(solution)/shard_map/all_to_all | solution.py:20
  404.7 2.7 convolution_convert_fusion.5
  410.0 3.5 all-to-all-start.8
  413.6 2.7 convolution_convert_fusion.3
  418.4 2.6 convolution_convert_fusion.4
  421.1 2.7 all_to_all.120
  428.3 4.7 all-to-all-start.9
  433.6 41.6 %all-gather.10.cloned.1.call-done = bf16[2031616]{0:T(1024)(128)(2,1)} async-done(((bf16[253952]{0:T(1024)(128)(2,1)}), bf16[2031616]{0:T(1024)(128)(2,1)}) %all-gather.10.cloned.1.call-update) | async-done | bytes 4063248 | tf_op jit(solution)/shard_map/all_gather | solution.py:38
  475.1 5.8 reshape.331
  485.7 2.7 slice.99
  488.4 3.0 reshape.362
  491.4 4.6 reshape.275
  496.0 3.8 copy.155
  502.2 2.8 reshape.364
  505.0 5.2 reshape.273
  510.2 3.7 copy.154
  513.9 3.3 reshape.366
  517.2 4.1 reshape.271
  521.4 3.9 copy.153
  525.3 2.6 convolution_bitcast_fusion.2
  529.1 4.2 all-to-all-start.7
  537.4 7.7 all-to-all-done.7
  545.1 4.3 all-to-all-start.5
  553.2 13.9 %all-to-all-done.5 = bf16[8,64,1280]{2,1,0:T(8,128)(2,1)} async-done(((bf16[8,64,1280]{2,1,0:T(8,128)(2,1)}), bf16[8,64,1280]{2,1,0:T(8,128)(2,1)}, u32[]{:S(2)}, u32[]{:S(2)}) %all-to-all-start.5) | async-done | bytes 1310752 | tf_op jit(solution)/shard_map/all_to_all | solution.py:58
  572.0 4.4 all-to-all-start.6
  576.7 3.6 fusion.3
  580.3 4.9 copy.167
  585.2 6.0 reshape.356
  591.3 4.4 all-to-all-done.6
  595.7 4.0 convolution_convert_fusion
  599.8 5.8 convolution_convert_fusion.1
  605.6 3.9 pad_maximum_fusion
  609.5 5.7 copy.165
  618.3 61.0 %reduce-scatter.20.cloned.1.call-done = bf16[96,160]{1,0:T(8,128)(2,1)} async-done(((bf16[1536,160]{1,0:T(8,128)(2,1)}), bf16[96,160]{1,0:T(8,128)(2,1)}) %reduce-scatter.20.cloned.1.call-update) | async-done | bytes 30736
  680.9 62.4 %reduce-scatter.18.cloned.1.call-done = bf16[80,480]{1,0:T(8,128)(2,1)} async-done(((bf16[1280,480]{1,0:T(8,128)(2,1)}), bf16[80,480]{1,0:T(8,128)(2,1)}) %reduce-scatter.18.cloned.1.call-update) | async-done | bytes 76816
  745.3 65.1 %reduce-scatter.16.cloned.1.call-done = bf16[80,1280]{1,0:T(8,128)(2,1)} async-done(((bf16[1280,1280]{1,0:T(8,128)(2,1)}), bf16[80,1280]{1,0:T(8,128)(2,1)}) %reduce-scatter.16.cloned.1.call-update) | async-done | bytes 204816
  (205 shorter events, 142.2 us)
Async XLA Ops:
  7.2 6.1 copy-start
  7.2 1.8 copy-start.2
  7.2 2.3 copy-start.28
  7.2 231.7 %all-gather.8.cloned.1.call-start = ((), (), s32[]{:S(2)}) async-start(), calls=%async_computation.17 | async-start | bytes 23592960 | tf_op jit(solution)/shard_map/all_gather | solution.py:181
  9.0 3.2 copy-start.22
  9.5 2.7 copy-start.26
  12.2 1.1 copy-start.31
  16.3 349.8 %all-gather.6.cloned.1.call-start = ((), (), s32[]{:S(2)}) async-start(), calls=%async_computation.15 | async-start | bytes 4423680 | tf_op jit(solution)/shard_map/all_gather | solution.py:187
  248.6 2.5 copy-start.1
  251.7 1.3 copy-start.14
  251.7 1.3 copy-start.20
  252.2 1.6 copy-start.3
  253.8 1.0 copy-start.4
  253.8 2.1 copy-start.13
  255.9 4.7 copy-start.25
  257.0 47.4 %all-to-all-start.2 = ((bf16[160,8,144]{0,2,1:T(8,128)(2,1)}), bf16[160,8,144]{0,2,1:T(8,128)(2,1)S(1)}, u32[]{:S(2)}, u32[]{:S(2)}) async-start(bf16[160,8,144]{0,2,1:T(8,128)(2,1)} %bitcast.155), calls=%async_computation.2 | async-start | bytes 1179648 | tf_op jit(solution)/shard_map/all_to_all | solution.py:190
  290.6 5.1 copy-start.21
  304.4 10.3 %copy-start.7 = (bf16[160,8,144]{0,2,1:T(8,128)(2,1)}, bf16[160,8,144]{0,2,1:T(8,128)(2,1)S(1)}, u32[]{:S(2)}) copy-start(bf16[160,8,144]{0,2,1:T(8,128)(2,1)S(1)} %all-to-all-done.2) | copy-start | bytes 1105924
  304.4 19.0 %all-to-all-start.3 = ((bf16[160,8,160]{0,2,1:T(8,128)(2,1)}), bf16[160,8,160]{0,2,1:T(8,128)(2,1)}, u32[]{:S(2)}, u32[]{:S(2)}) async-start(bf16[160,8,160]{0,2,1:T(8,128)(2,1)} %bitcast.152), calls=%async_computation.3 | async-start | bytes 1310720 | tf_op jit(solution)/shard_map/all_to_all | solution.py:191
  312.6 15.6 %copy-start.30 = (s32[16]{0:T(128)S(1)}, s32[16]{0:T(128)}, u32[]{:S(2)}) copy-start(s32[16]{0:T(128)} %get-tuple-element.15) | copy-start | bytes 196
  323.5 15.5 %all-to-all-start.1 = ((bf16[16,32,496]{2,1,0:T(8,128)(2,1)}), bf16[16,32,496]{2,1,0:T(8,128)(2,1)S(1)}, u32[]{:S(2)}, u32[]{:S(2)}) async-start(bf16[16,32,496]{2,1,0:T(8,128)(2,1)} %pad_maximum_fusion.1), calls=%async_computation.1 | async-start | bytes 1048576 | tf_op jit(solution)/shard_map/all_to_all | solution.py:14
  339.0 29.7 %all-to-all-start = ((bf16[160,8,192]{2,0,1:T(8,128)(2,1)}), bf16[160,8,192]{2,0,1:T(8,128)(2,1)}, u32[]{:S(2)}, u32[]{:S(2)}) async-start(bf16[160,8,192]{2,0,1:T(8,128)(2,1)} %copy.134), calls=%async_computation | async-start | bytes 1310720 | tf_op jit(solution)/shard_map/all_to_all | solution.py:189
  345.8 129.3 %all-gather.10.cloned.1.call-start = ((), (), s32[]{:S(2)}) async-start(), calls=%async_computation.18 | async-start | bytes 4571136 | tf_op jit(solution)/shard_map/all_gather | solution.py:38
  353.1 5.8 copy-start.8
  360.9 4.2 copy-start.9
  366.0 2.7 copy-start.12
  368.7 2.8 copy-start.16
  368.7 2.8 copy-start.19
  392.1 8.4 %copy-start.18 = (bf16[512,160]{0,1:T(8,128)(2,1)}, bf16[512,160]{0,1:T(8,128)(2,1)S(1)}, u32[]{:S(2)}) copy-start(bf16[512,160]{0,1:T(8,128)(2,1)S(1)} %subtract_convert_fusion.1) | copy-start | bytes 491524
  401.6 3.1 copy-start.17
  410.0 18.3 %all-to-all-start.8 = ((bf16[8,160,144]{1,2,0:T(8,128)(2,1)}), bf16[8,160,144]{1,2,0:T(8,128)(2,1)S(1)}, u32[]{:S(2)}, u32[]{:S(2)}) async-start(bf16[8,160,144]{1,2,0:T(8,128)(2,1)} %copy.158), calls=%async_computation.8 | async-start | bytes 1179648 | tf_op jit(solution)/shard_map/all_to_all | solution.py:214
  428.3 4.9 copy-start.6
  428.3 100.7 %all-to-all-start.9 = ((bf16[8,160,160]{1,2,0:T(8,128)(2,1)}), bf16[8,160,160]{1,2,0:T(8,128)(2,1)}, u32[]{:S(2)}, u32[]{:S(2)}) async-start(bf16[8,160,160]{1,2,0:T(8,128)(2,1)} %copy.159), calls=%async_computation.10 | async-start | bytes 1310720 | tf_op jit(solution)/shard_map/all_to_all | solution.py:214
  433.0 182.2 %reduce-scatter.14.cloned.1.call-start = ((), (), s32[]{:S(2)}) async-start(), calls=%async_computation.16 | async-start | bytes 626688 | tf_op jit(solution)/shard_map/reduce_scatter | solution.py:255
  496.0 3.8 copy-start.11
  521.4 6.5 copy-start.10
  525.3 2.6 copy-start.5
  529.1 16.1 %all-to-all-start.7 = ((bf16[8,160,192]{2,1,0:T(8,128)(2,1)}), bf16[8,160,192]{2,1,0:T(8,128)(2,1)}, u32[]{:S(2)}, u32[]{:S(2)}) async-start(bf16[8,160,192]{2,1,0:T(8,128)(2,1)} %bitcast.151), calls=%async_computation.7 | async-start | bytes 1310720 | tf_op jit(solution)/shard_map/all_to_all | solution.py:214
  533.3 2.2 copy-start.15
  545.1 21.9 %all-to-all-start.5 = ((bf16[8,64,1280]{2,1,0:T(8,128)(2,1)}), bf16[8,64,1280]{2,1,0:T(8,128)(2,1)}, u32[]{:S(2)}, u32[]{:S(2)}) async-start(bf16[8,64,1280]{2,1,0:T(8,128)(2,1)} %bitcast.159), calls=%async_computation.5 | async-start | bytes 2621440 | tf_op jit(solution)/shard_map/all_to_all | solution.py:58
  549.4 67.4 %reduce-scatter.22.cloned.1.call-start = ((), (), s32[]{:S(2)}) async-start(), calls=%async_computation.22 | async-start | bytes 696320
  550.0 129.3 %reduce-scatter.20.cloned.1.call-start = ((), (), s32[]{:S(2)}) async-start(), calls=%async_computation.21 | async-start | bytes 835584
  572.0 23.7 %all-to-all-start.6 = ((bf16[8,64,1280]{2,1,0:T(8,128)(2,1)}), bf16[8,64,1280]{2,1,0:T(8,128)(2,1)}, u32[]{:S(2)}, u32[]{:S(2)}) async-start(bf16[8,64,1280]{2,1,0:T(8,128)(2,1)} %broadcast_in_dim.32), calls=%async_computation.6 | async-start | bytes 2621440 | tf_op jit(solution)/shard_map/all_to_all | solution.py:20
  576.5 166.8 %reduce-scatter.18.cloned.1.call-start = ((), (), s32[]{:S(2)}) async-start(), calls=%async_computation.20 | async-start | bytes 1392640
  591.3 219.1 %reduce-scatter.16.cloned.1.call-start = ((), (), s32[]{:S(2)}) async-start(), calls=%async_computation.19 | async-start | bytes 3481600
  595.7 4.1 copy-start.23
  595.7 4.1 copy-start.27
  595.7 4.1 copy-start.29
  (1 other events, 0.6 us)
Sparse Core Ops, SparseCore 0:
  16.4 222.4 all-gather.7
  256.0 71.5 all-gather.5
  404.8 70.2 all-gather.9
  477.3 59.6 reduce-scatter.13
  552.3 64.4 reduce-scatter.21
  619.0 60.3 reduce-scatter.19
  681.7 61.5 reduce-scatter.17
  745.7 64.6 reduce-scatter.15
